TPU v7x, 32 devices: a whole 2x2x4 slice. The times are simulated.
32 devices in a mesh: occ: 16 (over z, y, x), blk: 2 (over core).
Axes of the slice: x: 2, y: 2, z: 4, core: 2. Of those that a mesh axis runs over, the one named last changes fastest.
Arguments:
- integrals: bfloat16 [20480, 16, 240], P(('occ', 'blk')), may hold values from -0.7 to 0.7
- domain_transforms: bfloat16 [32, 24, 24], replicated, may hold values from -1.25 to 1.25
- domain_lists: int32 [16, 2, 5], replicated, may hold values from 0 to 31, all different within a row
- occ_energies: float32 [16, 2, 1], P('occ'), may hold values from -1.5 to -0.4
- virt_energies: float32 [32, 24], replicated, may hold values from 0.3 to 2.5
- pair_pattern: int32 [16, 2, 2], P('occ'), may hold values from 0 to 1, as said below
Outputs:
- gradient_gamma: bfloat16 [20480, 16, 240], P(('occ', 'blk'))
Inputs may be any that keep to these rules, and one draw needn't show every extreme that they name: `domain_lists`: the 5 virtual blocks of each occupied block are distinct. `pair_pattern`: symmetric in its last two dimensions, with ones on the diagonal.
All inputs are finite; a program needn't handle non-finite values.
Results may differ from a plain program's by a relative error of at most 0.0049.
Values may be sent and summed in bfloat16 or wider, within the bound.
A program may use at most 128 MiB of HBM per device.

v0:
```python
import jax
import jax.numpy as jnp
from jax import lax
from jax.sharding import PartitionSpec as P

VB = 24
NDOM = 5
OB = 1


def build_fitted(raw_rows, transforms):
    row_count, group_count, width_all = raw_rows.shape
    block_count = transforms.shape[1]
    shaped = raw_rows.reshape(row_count, group_count, block_count, OB, NDOM, VB)
    mixed = jnp.einsum(
        "pgbomu,gbmuv->pgbomv", shaped, transforms, preferred_element_type=jnp.float32
    )
    return mixed.astype(jnp.bfloat16).reshape(row_count, group_count, width_all)


def on_device(
    integrals, domain_transforms, domain_lists, occ_energies, virt_energies, pair_pattern
):
    group_here = lax.axis_index("occ")
    own_lists = lax.dynamic_index_in_dim(domain_lists, group_here, 0, keepdims=True)
    every_transform = jnp.take(domain_transforms, domain_lists, axis=0)
    fitted_all = build_fitted(integrals, every_transform)
    fitted = lax.all_to_all(fitted_all, "occ", split_axis=1, concat_axis=0, tiled=True)
    aux_rows = fitted.shape[0]
    width_all = fitted.shape[2]
    fitted = fitted.reshape(aux_rows, width_all)
    block_count = pair_pattern.shape[1]
    width_block = width_all // block_count
    block_virt = jnp.take(virt_energies, own_lists[0], axis=0)
    col_energy = (occ_energies[0][:, :, None, None] - block_virt[:, None, :, :]).reshape(width_all)
    pattern_now = pair_pattern[0]
    pattern_float = pattern_now.astype(jnp.float32)
    mask_full = jnp.repeat(jnp.repeat(pattern_float, width_block, axis=0), width_block, axis=1)
    partial_sums = lax.dot_general(
        fitted, fitted, (((0,), (0,)), ((), ())), preferred_element_type=jnp.float32
    )
    row_sums = lax.psum_scatter(partial_sums, "blk", scatter_dimension=0, tiled=True)
    share_rows = row_sums.shape[0]
    block_here = lax.axis_index("blk")
    row_energy = lax.dynamic_slice_in_dim(col_energy, block_here * share_rows, share_rows, 0)
    row_mask = lax.dynamic_slice_in_dim(mask_full, block_here * share_rows, share_rows, 0)
    row_amplitudes = (row_mask * row_sums / (row_energy[:, None] + col_energy[None, :])).astype(
        jnp.bfloat16
    )
    amplitudes = lax.all_gather(row_amplitudes, "blk", axis=0, tiled=True)
    gamma_rows = lax.dot_general(
        fitted, amplitudes, (((1,), (1,)), ((), ())), preferred_element_type=jnp.float32
    )
    gamma_rows = gamma_rows.astype(jnp.bfloat16).reshape(aux_rows, 1, width_all)
    return lax.all_to_all(gamma_rows, "occ", split_axis=0, concat_axis=1, tiled=True)


def solution(mesh):
    return jax.shard_map(
        on_device,
        mesh=mesh,
        in_specs=(
            P(("occ", "blk"), None, None),
            P(),
            P(),
            P("occ", None, None),
            P(),
            P("occ", None, None),
        ),
        out_specs=P(("occ", "blk"), None, None),
        check_vma=False,
    )
```

profile of v0, /device:TPU:0, one launch (start us, length us, event | category | flops | bytes accessed | tf_op | source)
XLA Modules:
  0.0 350.3 jit_solution(12702951507838364540)
XLA Ops:
  6.5 0.7 compare_and_fusion
  7.2 0.7 compare_select_fusion
  7.9 0.1 copy.32
  8.1 0.1 copy.33
  8.2 0.1 reshape.104
  8.3 1.1 copy.34
  9.4 0.8 gather_fusion
  10.2 7.7 %convolution_convert_fusion.1 = bf16[16,2,5,24,640]{4,3,2,1,0:T(8,128)(2,1)} fusion(bf16[640,16,2,5,24]{0,4,3,2,1:T(8,128)(2,1)} %bitcast.50, bf16[16,2,5,24,24]{4,3,2,1,0:T(8,128)(2,1)S(1)} %bitcast.51, pred[16,2,5]{2,1,0:T(4,128)(4,1)S(1)} %copy.32), kind=kOutput, calls=%fused_computation.6 | convolution fusion | flops 120514560 | bytes 10014880 | tf_op jit(solution)/shard_map/pgbomu,gbmuv->pgbomv/dot_general | solution.py:15
  17.9 0.0 copy-start
  17.9 8.5 %all-to-all-start = ((bf16[640,16,240]{0,2,1:T(8,128)(2,1)}), bf16[640,16,240]{0,2,1:T(8,128)(2,1)}, u32[]{:S(2)}, u32[]{:S(2)}) async-start(bf16[640,16,240]{0,2,1:T(8,128)(2,1)} %bitcast.48), calls=%async_computation | async-start | bytes 9830400 | tf_op jit(solution)/shard_map/all_to_all | solution.py:28
  26.4 0.0 reduce-scatter.2.cloned.1.call-start
  26.5 0.0 copy-done
  26.5 0.1 constant_dynamic-slice_fusion
  26.6 0.1 copy.37
  26.7 0.1 reshape.112
  26.8 0.0 copy-start.3
  26.8 0.0 copy-start.1
  26.8 0.0 copy-start.2
  26.8 92.5 %all-to-all-done = bf16[640,16,240]{0,2,1:T(8,128)(2,1)} async-done(((bf16[640,16,240]{0,2,1:T(8,128)(2,1)}), bf16[640,16,240]{0,2,1:T(8,128)(2,1)}, u32[]{:S(2)}, u32[]{:S(2)}) %all-to-all-start) | async-done | bytes 4915232 | tf_op jit(solution)/shard_map/all_to_all | solution.py:28
  119.3 6.0 %fusion.3 = f32[240,240]{1,0:T(8,128)} fusion(bf16[640,16,240]{0,2,1:T(8,128)(2,1)} %all-to-all-done), kind=kOutput, calls=%fused_computation.7 | convolution fusion | flops 1179648000 | bytes 5145600 | tf_op jit(solution)/shard_map/dot_general | solution.py:39
  125.4 0.0 reduce-scatter.2.cloned.1.call-update
  125.4 0.1 broadcast_in_dim.37
  125.5 0.1 broadcast_in_dim.38
  125.6 0.0 copy-done.3
  125.6 0.1 sub.20
  125.7 0.1 sub.21
  125.7 0.0 copy-done.1
  125.7 0.1 copy.39
  125.8 0.6 gather_fusion.1
  126.4 0.1 gather.12
  126.5 0.0 copy-done.2
  126.5 0.3 broadcast_in_dim.36
  126.8 0.2 reshape.99
  127.0 0.1 dynamic_slice.12
  127.1 5.4 %copy.47 = bf16[30,8,16,640]{3,1,2,0:T(8,128)(2,1)} copy(bf16[30,8,16,640]{3,1,0,2:T(8,128)(2,1)} %bitcast.40) | data formatting | bytes 9830400
  132.5 18.3 %reduce-scatter.2.cloned.1.call-done = f32[120,240]{1,0:T(8,128)} async-done(((f32[240,240]{1,0:T(8,128)}), f32[120,240]{1,0:T(8,128)}) %reduce-scatter.2.cloned.1.call-update) | async-done | bytes 115216 | tf_op jit(solution)/shard_map/reduce_scatter | solution.py:42
  150.8 1.0 divide_convert_fusion
  151.8 1.9 all_gather.3
  153.7 6.0 %fusion = bf16[10240,1,240]{0,2,1:T(8,128)(2,1)} fusion(bf16[240,240]{1,0:T(8,128)(2,1)S(1)} %all_gather.3, bf16[10240,240]{0,1:T(8,128)(2,1)} %bitcast.49), kind=kOutput, calls=%fused_computation.3 | convolution fusion | flops 1182105600 | bytes 9945600 | tf_op jit(solution)/shard_map/dot_general | solution.py:51
  159.7 0.5 broadcast.60
  160.2 7.5 %reduce = bf16[10240,240]{0,1:T(8,128)(2,1)} reduce(bf16[10240,1,240]{0,2,1:T(8,128)(2,1)} %fusion, bf16[]{:T(256)} %broadcast.60), dimensions={1}, to_apply=%copy.40.reduce_sub_computation | reduce | bytes 9830402 | tf_op jit(solution)/shard_map/reshape | solution.py:54
  167.7 7.8 %copy.49 = bf16[10240,240]{1,0:T(8,128)(2,1)} copy(bf16[10240,240]{0,1:T(8,128)(2,1)} %reduce) | data formatting | bytes 9830400
  175.6 15.3 %reshape.124 = bf16[16,2,76800]{2,1,0:T(2,128)(2,1)} reshape(bf16[10240,240]{1,0:T(8,128)(2,1)} %copy.49) | data formatting | bytes 9830400
  190.9 117.2 %all_to_all.33 = bf16[16,2,76800]{2,1,0:T(2,128)(2,1)} all-to-all(bf16[16,2,76800]{2,1,0:T(2,128)(2,1)} %reshape.124), channel_id=1, replica_groups=mesh['occ'=16,'blk'=2] {'occ'}, dimensions={0} | all-to-all | bytes 9830400 | tf_op jit(solution)/shard_map/all_to_all | solution.py:55
  308.1 19.6 %reshape.125 = bf16[10240,1,240]{2,1,0:T(2,128)(2,1)} reshape(bf16[16,2,76800]{2,1,0:T(2,128)(2,1)} %all_to_all.33) | data formatting | bytes 9830400
  327.7 8.0 %copy.46 = bf16[10240,1,240]{2,0,1:T(8,128)(2,1)} copy(bf16[10240,1,240]{2,1,0:T(2,128)(2,1)} %reshape.125) | data formatting | bytes 9830400
  335.8 7.7 %copy.42 = bf16[640,16,240]{0,2,1:T(8,128)(2,1)} copy(bf16[640,16,240]{2,0,1:T(8,128)(2,1)} %bitcast.47) | data formatting | bytes 9830400 | tf_op jit(solution)/shard_map/all_to_all | solution.py:55
  (7 shorter events, 0.0 us)
Async XLA Ops:
  17.9 8.6 %copy-start = (s32[16,2,5]{0,1,2:T(2,128)S(1)}, s32[16,2,5]{0,1,2:T(2,128)}, u32[]{:S(2)}) copy-start(s32[16,2,5]{0,1,2:T(2,128)} %param.8) | copy-start | bytes 1924
  17.9 101.4 %all-to-all-start = ((bf16[640,16,240]{0,2,1:T(8,128)(2,1)}), bf16[640,16,240]{0,2,1:T(8,128)(2,1)}, u32[]{:S(2)}, u32[]{:S(2)}) async-start(bf16[640,16,240]{0,2,1:T(8,128)(2,1)} %bitcast.48), calls=%async_computation | async-start | bytes 9830400 | tf_op jit(solution)/shard_map/all_to_all | solution.py:28
  26.4 124.4 %reduce-scatter.2.cloned.1.call-start = ((), (), s32[]{:S(2)}) async-start(), calls=%async_computation.3 | async-start | bytes 368640 | tf_op jit(solution)/shard_map/reduce_scatter | solution.py:42
  26.8 98.8 %copy-start.3 = (f32[1,2,1]{1,2,0:T(1,128)S(1)}, f32[1,2,1]{1,2,0:T(1,128)}, u32[]{:S(2)}) copy-start(f32[1,2,1]{1,2,0:T(1,128)} %param.9) | copy-start | bytes 28
  26.8 99.0 %copy-start.1 = (f32[32,24]{0,1:T(8,128)S(1)}, f32[32,24]{0,1:T(8,128)}, u32[]{:S(2)}) copy-start(f32[32,24]{0,1:T(8,128)} %param.10) | copy-start | bytes 9220
  26.8 99.7 %copy-start.2 = (s32[1,2,2]{2,1,0:T(2,128)S(1)}, s32[1,2,2]{2,1,0:T(2,128)}, u32[]{:S(2)}) copy-start(s32[1,2,2]{2,1,0:T(2,128)} %param.11) | copy-start | bytes 52
Sparse Core Ops, SparseCore 0:
  125.5 25.2 reduce-scatter.1
where the time goes:
time: 352 us; the launch traced here: 350 us
  blocking collectives  119 us (34%)
  waiting for transfers between devices  111 us (32%)
  local copies, waits for them, and re-layouts  68.5 us (19%)
  matrix products  19.8 us (6%)
  between operations  13.5 us (4%)
  other arithmetic  9.92 us (3%)
  starting transfers between devices  8.56 us (2%)
    all_to_all x1, blocking collectives, on_device(): lax.all_to_all(gamma_rows, 'occ', split_axis=0, concat_axis=1, tiled=True)  117 us
    all_to_all x1, waiting for transfers between devices, on_device(): lax.all_to_all(fitted_all, 'occ', split_axis=1, concat_axis=0, tiled=True)  92.5 us
    unnamed x15, local copies, waits for them, and re-layouts  57.3 us
    reduce_scatter x1, waiting for transfers between devices, on_device(): lax.psum_scatter(partial_sums, 'blk', scatter_dimension=0, tiled=True)  18.3 us
    all_to_all x1, starting transfers between devices, on_device(): lax.all_to_all(fitted_all, 'occ', split_axis=1, concat_axis=0, tiled=True)  8.52 us
    dot_general x1, matrix products, build_fitted(): jnp.einsum('pgbomu,gbmuv->pgbomv', shaped, transforms, preferred_element_...  7.72 us
    all_to_all x1, local copies, waits for them, and re-layouts, on_device(): lax.all_to_all(gamma_rows, 'occ', split_axis=0, concat_axis=1, tiled=True)  7.71 us
    reshape x1, other arithmetic, on_device(): gamma_rows = gamma_rows.astype(jnp.bfloat16).reshape(aux_rows, 1, width_all)  7.5 us
  transfers between devices with their start and end apart: 2, of which 2 were waited for; matrix products, arithmetic and copies ran while one was open for 2% of the time, Pallas kernels for 0%

commit v1 on v0

--- a/solution.py
+++ b/solution.py
@@ -1,3 +1,4 @@
+import functools
 import jax
 import jax.numpy as jnp
 from jax import lax
@@ -6,6 +7,17 @@
 VB = 24
 NDOM = 5
 OB = 1
+
+
+def finish_weights(x_in, group_axis):
+    e_now = jax.lax.axis_size(group_axis)
+    local_out = jnp.split(x_in, e_now, 0)
+    far_arr = jnp.stack(local_out, 0)
+    back = jax.lax.all_to_all(far_arr, group_axis, 0, 0)
+    return jnp.concatenate(back, 1)
+
+
+point_forms_on_mesh = functools.partial(finish_weights, group_axis="occ")
 
 
 def build_fitted(raw_rows, transforms):
@@ -52,7 +64,7 @@
         fitted, amplitudes, (((1,), (1,)), ((), ())), preferred_element_type=jnp.float32
     )
     gamma_rows = gamma_rows.astype(jnp.bfloat16).reshape(aux_rows, 1, width_all)
-    return lax.all_to_all(gamma_rows, "occ", split_axis=0, concat_axis=1, tiled=True)
+    return point_forms_on_mesh(gamma_rows)
 
 
 def solution(mesh):

time: 352 us -> 279 us (0.79)
  blocking collectives: 119 us -> 235 us
  waiting for transfers between devices: 111 us -> 0.02 us
  local copies, waits for them, and re-layouts: 68.5 us -> 15.4 us
  starting transfers between devices: 8.56 us -> 0.01 us
  matrix products: 19.8 us -> 11.5 us
  other arithmetic: 9.92 us -> 2.41 us
    all_to_all x1 -> x2, blocking collectives: 117 us -> 233 us  [the longest x1 118 us: on_device(): lax.all_to_all(fitted_all, 'occ', split_axis=1, concat_axis=0, tiled=True)]
    all_to_all x1 -> x0, waiting for transfers between devices: 92.5 us -> none  [on_device(): lax.all_to_all(fitted_all, 'occ', split_axis=1, concat_axis=0, tiled=True)]
    unnamed x15 -> x27, local copies, waits for them, and re-layouts: 57.3 us -> 11.7 us
    reduce_scatter x1, waiting for transfers between devices: 18.3 us -> 0.01 us  [on_device(): lax.psum_scatter(partial_sums, 'blk', scatter_dimension=0, tiled=True)]
    all_to_all x1 -> x0, starting transfers between devices: 8.52 us -> none  [on_device(): lax.all_to_all(fitted_all, 'occ', split_axis=1, concat_axis=0, tiled=True)]
    all_to_all x1 -> x0, local copies, waits for them, and re-layouts: 7.71 us -> none  [on_device(): lax.all_to_all(gamma_rows, 'occ', split_axis=0, concat_axis=1, tiled=True)]
    reshape x1 -> x0, other arithmetic: 7.5 us -> none  [on_device(): gamma_rows = gamma_rows.astype(jnp.bfloat16).reshape(aux_rows, 1, width_all)]
    dot_general x1, matrix products: 6.05 us -> 2.16 us  [on_device(): lax.dot_general(fitted, fitted, (((0,), (0,)), ((), ())), preferred_eleme...]
  transfers between devices with their start and end apart: 2 -> 1, of which waited for: 2 -> 0; matrix products, arithmetic and copies ran while one was open for 2% -> 3% of each run, Pallas kernels for 0% -> 0%
where the time goes in v1:
time: 279 us; the launch traced here: 278 us
  blocking collectives  235 us (84%)
  local copies, waits for them, and re-layouts  15.4 us (6%)
  between operations  13.6 us (5%)
  matrix products  11.5 us (4%)
    all_to_all x1, blocking collectives, on_device(): lax.all_to_all(fitted_all, 'occ', split_axis=1, concat_axis=0, tiled=True)  118 us
    all_to_all x1, blocking collectives, finish_weights(): back = jax.lax.all_to_all(far_arr, group_axis, 0, 0)  115 us
    unnamed x27, local copies, waits for them, and re-layouts  11.7 us
  transfers between devices with their start and end apart: 1, of which 0 were waited for; matrix products, arithmetic and copies ran while one was open for 3% of the time, Pallas kernels for 0%

profile of v1, /device:TPU:0, one launch (start us, length us, event | category | flops | bytes accessed | tf_op | source)
XLA Modules:
  0.0 278.1 jit_solution(6256943412401552125)
XLA Ops:
  6.5 0.0 reduce-scatter.2.cloned.1.call-start
  6.5 0.7 compare_and_fusion
  7.2 0.7 compare_select_fusion
  7.9 0.8 constant_dynamic-slice_fusion
  8.7 0.1 copy.25
  8.8 0.1 reshape.149
  8.9 0.1 copy.20
  9.0 0.1 copy.21
  9.1 0.1 reshape.141
  9.2 1.1 copy.22
  10.3 0.8 gather_fusion
  11.2 5.5 %convolution_convert_fusion.1 = bf16[16,2,5,24,640]{4,3,2,1,0:T(8,128)(2,1)S(1)} fusion(bf16[640,16,2,5,24]{0,4,3,2,1:T(8,128)(2,1)} %bitcast.111, bf16[16,2,5,24,24]{4,3,2,1,0:T(8,128)(2,1)S(1)} %bitcast.112, pred[16,2,5]{2,1,0:T(4,128)(4,1)S(1)} %copy.20), kind=kOutput, calls=%fused_computation.5 | convolution fusion | flops 120514560 | bytes 10014880 | tf_op jit(solution)/shard_map/pgbomu,gbmuv->pgbomv/dot_general | solution.py:27
  16.6 118.0 %all_to_all.20 = bf16[640,16,240]{0,2,1:T(8,128)(2,1)S(1)} all-to-all(bf16[640,16,240]{0,2,1:T(8,128)(2,1)S(1)} %bitcast.109), channel_id=1, replica_groups=mesh['occ'=16,'blk'=2] {'occ'}, dimensions={1} | all-to-all | bytes 9830400 | tf_op jit(solution)/shard_map/all_to_all | solution.py:40
  134.7 0.0 copy-start
  134.7 2.2 copy-done
  136.9 0.0 copy-start.3
  136.9 0.0 copy-start.1
  136.9 0.0 copy-start.2
  136.9 2.2 fusion.2
  139.1 0.0 reduce-scatter.2.cloned.1.call-update
  139.1 0.1 broadcast_in_dim.37
  139.2 0.1 broadcast_in_dim.38
  139.3 0.0 copy-done.3
  139.3 0.1 sub.20
  139.4 0.1 sub.21
  139.4 0.0 copy-done.1
  139.5 0.1 copy.27
  139.5 0.6 gather_fusion.1
  140.1 0.1 gather.12
  140.2 0.0 copy-done.2
  140.2 0.3 broadcast_in_dim.36
  140.5 0.2 reshape.135
  140.7 0.1 dynamic_slice.12
  140.8 5.4 %copy.29 = bf16[30,8,16,640]{3,1,2,0:T(8,128)(2,1)} copy(bf16[30,8,16,640]{3,1,0,2:T(8,128)(2,1)} %bitcast.108) | data formatting | bytes 9830400
  146.2 0.0 reduce-scatter.2.cloned.1.call-done
  146.2 1.0 divide_convert_fusion
  147.2 1.9 all_gather.3
  149.1 3.8 %convolution_convert_fusion = bf16[10240,240]{0,1:T(8,128)(2,1)S(1)} fusion(bf16[240,240]{1,0:T(8,128)(2,1)S(1)} %all_gather.3, bf16[10240,240]{0,1:T(8,128)(2,1)} %bitcast.107), kind=kOutput, calls=%fused_computation.2 | convolution fusion | flops 1182105600 | bytes 9945600 | tf_op jit(solution)/shard_map/dot_general | solution.py:63
  153.7 115.3 %all_to_all.21 = bf16[16,640,1,240]{1,3,2,0:T(8,128)(2,1)S(1)} all-to-all(bf16[16,640,1,240]{1,3,2,0:T(8,128)(2,1)S(1)} %fusion.8), channel_id=1, replica_groups=mesh['occ'=16,'blk'=2] {'occ'}, dimensions={0} | all-to-all | bytes 9830400 | tf_op jit(solution)/shard_map/all_to_all | solution.py:16
  269.0 2.3 copy.47
  (22 shorter events, 0.7 us)
Async XLA Ops:
  6.5 139.7 %reduce-scatter.2.cloned.1.call-start = ((), (), s32[]{:S(2)}) async-start(), calls=%async_computation.3 | async-start | bytes 368640 | tf_op jit(solution)/shard_map/reduce_scatter | solution.py:54
  134.7 2.3 copy-start
  136.9 2.4 copy-start.3
  136.9 2.5 copy-start.1
  136.9 3.3 %copy-start.2 = (s32[1,2,2]{2,1,0:T(2,128)S(1)}, s32[1,2,2]{2,1,0:T(2,128)}, u32[]{:S(2)}) copy-start(s32[1,2,2]{2,1,0:T(2,128)} %param.11) | copy-start | bytes 52
Sparse Core Ops, SparseCore 0:
  139.2 5.2 reduce-scatter.1
